TPU v7x, 256 devices: a whole 4x4x8 slice. The times are simulated.
256 devices in a mesh: wide: 64 (over z, y, core), narrow: 4 (over x).
Axes of the slice: x: 4, y: 4, z: 8, core: 2. Of those that a mesh axis runs over, the one named last changes fastest.
Arguments:
- hidden_in: bfloat16 [1024, 4096], P('narrow', 'wide'), may hold values from -0.59765625 to 0.59765625
- cached_len: int32 [4], replicated, may hold values from 1 to 4096, 8192 in all
- k_cache: bfloat16 [4, 32768, 128], P('narrow', 'wide'), may hold values from -256 to 256
- v_cache: bfloat16 [4, 32768, 128], P('narrow', 'wide'), may hold values from -24 to 24
- attn_gain: bfloat16 [4096], replicated, may hold values from 0.099609375 to 1.8984375
- ffn_gain: bfloat16 [4096], replicated, may hold values from 0.099609375 to 1.8984375
- wqkv: bfloat16 [6144, 4096], P('wide', 'narrow'), may hold values from -0.09375 to 0.09375
- wo: bfloat16 [4096, 4096], P('wide', 'narrow'), may hold values from -0.09375 to 0.09375
- wgate: bfloat16 [14336, 4096], P('wide', 'narrow'), may hold values from -0.09375 to 0.09375
- wup: bfloat16 [14336, 4096], P('wide', 'narrow'), may hold values from -0.09375 to 0.09375
- wdown: bfloat16 [14336, 4096], P('wide', 'narrow'), may hold values from -0.125 to 0.125
Outputs:
- hidden_out: bfloat16 [1024, 4096], P('narrow', 'wide')
- new_k_cache: bfloat16 [4, 32768, 128], P('narrow', 'wide')
- new_v_cache: bfloat16 [4, 32768, 128], P('narrow', 'wide')
All inputs are finite; a program needn't handle non-finite values.
Results may differ from a plain program's by a relative error of at most 0.018.
The roundings to bfloat16 on the way count: a program that leaves them out, or rounds other values in their place, can miss the bound.
Values may be sent and summed in bfloat16 or wider, within the bound.
A program may use at most 64 MiB of HBM per device.

v0:
```python
import jax
import jax.numpy as jnp
from jax import lax
from jax.sharding import PartitionSpec as P

QH = 32
KVH = 8
HD = 128
WINDOW = 4096
NEG_FILL = -1e30


def partner(block, axis, stride):
    count = lax.axis_size(axis)
    route = []
    for low in range(count):
        high = low | 1 << stride
        if high != low and high < count:
            route += [(low, high), (high, low)]
    return lax.ppermute(block, axis, route)


def rms_scale(values, weights):
    widened = values.astype(jnp.float32)
    mean_square = jnp.mean(widened * widened, axis=-1, keepdims=True)
    return (widened * lax.rsqrt(mean_square + 1e-05) * weights.astype(jnp.float32)).astype(
        jnp.bfloat16
    )


def times_rows(left, right):
    return lax.dot_general(
        left, right, (((1,), (1,)), ((), ())), preferred_element_type=jnp.float32
    )


def rotate(heads, positions):
    half_width = heads.shape[-1] // 2
    exponent = jnp.arange(half_width, dtype=jnp.float32) * (2.0 / heads.shape[-1])
    frequency = jnp.power(10000.0, -exponent)
    angles = positions.astype(jnp.float32)[:, None] * frequency[None, :]
    cosine = jnp.cos(angles)[:, None, :]
    sine = jnp.sin(angles)[:, None, :]
    widened = heads.astype(jnp.float32)
    first_half = widened[..., :half_width]
    second_half = widened[..., half_width:]
    return jnp.concatenate(
        [first_half * cosine - second_half * sine, second_half * cosine + first_half * sine],
        axis=-1,
    ).astype(jnp.bfloat16)


def gather_cols(block):
    return lax.all_gather(block, "wide", axis=1, tiled=True)


def collect_heads(qkv_piece, sections):
    position = lax.axis_index("wide")
    for bit_index in range(sections):
        other_piece = partner(qkv_piece, "wide", bit_index)
        upper_half = position // 2**bit_index % 2 == 1
        qkv_piece = jnp.where(
            upper_half,
            jnp.concatenate([other_piece, qkv_piece], axis=1),
            jnp.concatenate([qkv_piece, other_piece], axis=1),
        )
    return qkv_piece


def combine(earlier, later):
    highest = jnp.maximum(earlier[0], later[0])
    left_scale = jnp.exp(earlier[0] - highest)
    right_scale = jnp.exp(later[0] - highest)
    return (
        highest,
        earlier[1] * left_scale + later[1] * right_scale,
        earlier[2] * left_scale[..., None] + later[2] * right_scale[..., None],
    )


def empty_state(row_count, group_size):
    return (
        jnp.full((row_count, group_size), NEG_FILL, jnp.float32),
        jnp.zeros((row_count, group_size), jnp.float32),
        jnp.zeros((row_count, group_size, HD), jnp.float32),
    )


def attend(queries, query_pos, keys, values, key_pos, key_live, soft_state):
    row_count, group_size, head_width = queries.shape
    flat_queries = queries.reshape(row_count * group_size, head_width)
    key_count = keys.shape[0]
    block_size = min(512, key_count)
    block_count = key_count // block_size
    lowest = jnp.min(query_pos)
    highest = jnp.max(query_pos)

    def key_step(carry, blocks):
        key_block, value_block, pos_block, live_block = blocks

        def score_block(running):
            peak_old, totals, accum = running
            scores = jnp.einsum(
                "qd,kd->qk", flat_queries, key_block, preferred_element_type=jnp.float32
            )
            scores = scores.reshape(row_count, group_size, block_size) * HD ** (-0.5)
            allowed = (
                live_block[None, :]
                & (pos_block[None, :] <= query_pos[:, None])
                & (pos_block[None, :] > query_pos[:, None] - WINDOW)
            )
            allowed = allowed[:, None, :]
            scores = jnp.where(allowed, scores, NEG_FILL)
            peak_new = jnp.maximum(peak_old, jnp.max(scores, axis=-1))
            factor = jnp.exp(peak_old - peak_new)
            exp_terms = jnp.where(allowed, jnp.exp(scores - peak_new[..., None]), 0.0)
            totals = totals * factor + jnp.sum(exp_terms, axis=-1)
            weights = exp_terms.astype(jnp.bfloat16).reshape(row_count * group_size, block_size)
            mixed = jnp.dot(weights, value_block, preferred_element_type=jnp.float32).reshape(
                row_count, group_size, head_width
            )
            return (peak_new, totals, accum * factor[..., None] + mixed)

        useful = jnp.any(live_block & (pos_block <= highest) & (pos_block > lowest - WINDOW))
        return (lax.cond(useful, score_block, lambda unchanged: unchanged, carry), None)

    blocks = (
        keys.reshape(block_count, block_size, head_width),
        values.reshape(block_count, block_size, head_width),
        key_pos.reshape(block_count, block_size),
        key_live.reshape(block_count, block_size),
    )
    soft_state, _ = lax.scan(key_step, soft_state, blocks)
    return soft_state


def per_device(
    hidden_in, cached_len, k_cache, v_cache, attn_gain, ffn_gain, wqkv, wo, wgate, wup, wdown
):
    qkv_full, out_full, gate_full, up_full, down_full = (
        lax.all_gather(wqkv, "narrow", axis=1, tiled=True),
        lax.all_gather(wo, "narrow", axis=1, tiled=True),
        lax.all_gather(wgate, "narrow", axis=1, tiled=True),
        lax.all_gather(wup, "narrow", axis=1, tiled=True),
        lax.all_gather(wdown, "narrow", axis=1, tiled=True),
    )
    wide_count = lax.axis_size("wide")
    part_count = wide_count // KVH
    sections = part_count.bit_length() - 1
    position = lax.axis_index("wide")
    part_index = position % part_count
    length = cached_len[lax.axis_index("narrow")]
    span_len = hidden_in.shape[0]
    group_size = QH // KVH
    steps_t = jnp.arange(span_len, dtype=jnp.int32)
    query_pos = length + steps_t
    normed_attn = rms_scale(gather_cols(hidden_in), attn_gain)
    qkv_piece = times_rows(normed_attn, qkv_full).astype(jnp.bfloat16)
    grouped = collect_heads(qkv_piece, sections)
    queries = rotate(grouped[:, : group_size * HD].reshape(span_len, group_size, HD), query_pos)
    new_keys = rotate(
        grouped[:, group_size * HD : (group_size + 1) * HD].reshape(span_len, 1, HD), query_pos
    ).reshape(span_len, HD)
    new_vals = grouped[:, (group_size + 1) * HD :]
    cache_keys = k_cache[0]
    cache_vals = v_cache[0]
    block_slots = cache_keys.shape[0]
    slot_pos = part_index * block_slots + jnp.arange(block_slots, dtype=jnp.int32)
    share_rows = span_len // part_count
    start_row = part_index * share_rows
    soft_state = empty_state(span_len, group_size)
    soft_state = attend(
        queries, query_pos, cache_keys, cache_vals, slot_pos, slot_pos < length, soft_state
    )
    soft_state = attend(
        queries,
        query_pos,
        lax.dynamic_slice_in_dim(new_keys, start_row, share_rows, 0),
        lax.dynamic_slice_in_dim(new_vals, start_row, share_rows, 0),
        lax.dynamic_slice_in_dim(query_pos, start_row, share_rows, 0),
        jnp.ones((share_rows,), jnp.bool_),
        soft_state,
    )
    for bit_index in range(sections):
        soft_state = combine(soft_state, partner(soft_state, "wide", bit_index))
    attended = (
        (soft_state[2] / soft_state[1][..., None])
        .astype(jnp.bfloat16)
        .reshape(span_len, group_size * HD)
    )
    width_share = group_size * HD // part_count
    own_cols = lax.dynamic_slice_in_dim(attended, part_index * width_share, width_share, 1)
    mixed_heads = gather_cols(own_cols)
    projected = times_rows(mixed_heads, out_full)
    after_attn = (hidden_in.astype(jnp.float32) + projected).astype(jnp.bfloat16)
    whole_after = gather_cols(after_attn)
    normed_ffn = rms_scale(whole_after, ffn_gain)
    gate_proj = times_rows(normed_ffn, gate_full)
    up_proj = times_rows(normed_ffn, up_full)
    activation = (jax.nn.silu(gate_proj) * up_proj).astype(jnp.bfloat16)
    summed = lax.psum_scatter(
        lax.dot_general(
            down_full, activation, (((0,), (1,)), ((), ())), preferred_element_type=jnp.float32
        ),
        "wide",
        scatter_dimension=0,
        tiled=True,
    )
    hidden_out = (after_attn.astype(jnp.float32) + summed.T).astype(jnp.bfloat16)
    offset = (slot_pos - length) % WINDOW
    fresh_slot = offset < span_len
    pick_row = jnp.minimum(offset, span_len - 1)
    new_k_cache = jnp.where(fresh_slot[:, None], jnp.take(new_keys, pick_row, axis=0), cache_keys)[
        None
    ]
    new_v_cache = jnp.where(fresh_slot[:, None], jnp.take(new_vals, pick_row, axis=0), cache_vals)[
        None
    ]
    return (hidden_out, new_k_cache, new_v_cache)


def solution(mesh):
    return jax.shard_map(
        per_device,
        mesh=mesh,
        in_specs=(
            P("narrow", "wide"),
            P(),
            P("narrow", "wide", None),
            P("narrow", "wide", None),
            P(),
            P(),
            P("wide", "narrow"),
            P("wide", "narrow"),
            P("wide", "narrow"),
            P("wide", "narrow"),
            P("wide", "narrow"),
        ),
        out_specs=(P("narrow", "wide"), P("narrow", "wide", None), P("narrow", "wide", None)),
        check_vma=False,
    )
```

profile of v0, /device:TPU:2, one launch (start us, length us, event | category | flops | bytes accessed | tf_op | source)
XLA Modules:
  0.0 569.9 jit_solution(13301387686112721194)
XLA Ops:
  7.2 0.7 all-gather.7.cloned.1.call-update
  8.0 1.3 dynamic_slice.37
  9.2 1.2 fusion.63
  10.5 1.2 fusion.64
  11.7 0.7 convert_element_type.93
  13.1 2.0 fusion.58
  15.0 0.6 iota_add_fusion.1
  15.7 14.4 %all_gather.25 = bf16[96,4096]{1,0:T(8,128)(2,1)S(1)} all-gather(bf16[96,1024]{1,0:T(8,128)(2,1)} %param.23), channel_id=1, replica_groups=mesh['wide'=64,'narrow'=4] {'narrow'}, dimensions={1}, use_global_device_ids=true | all-gather | bytes 983040 | tf_op jit(solution)/shard_map/all_gather | solution.py:141
  30.1 61.0 %all-gather.7.cloned.1.call-done = bf16[256,4096]{0,1:T(8,128)(2,1)} async-done(((bf16[256,64]{0,1:T(8,128)(2,1)}), bf16[256,4096]{0,1:T(8,128)(2,1)}) %all-gather.7.cloned.1.call-update) | async-done | bytes 2097168 | tf_op jit(solution)/shard_map/all_gather | solution.py:54
  91.0 2.3 fusion.16
  93.4 0.8 fusion.27
  94.2 0.4 collective-permute-start
  94.6 1.9 and_reduce_fusion
  97.9 0.7 broadcast_in_dim.114
  98.5 0.6 collective-permute-start.1
  99.2 4.4 collective-permute-done.1
  103.6 2.2 collective-permute-start.2
  106.1 5.3 collective-permute-done.2
  111.6 0.6 fusion.69
  113.1 0.6 pad_maximum_fusion.1
  113.9 11.8 %conditional.2 = ((f32[256,4]{1,0:T(8,128)S(1)}, f32[256,4]{1,0:T(8,128)}, f32[256,4,128]{2,0,1:T(8,128)S(1)})) conditional(s32[]{:T(128)} %convert_element_type.91, (f32[256,4]{1,0:T(8,128)S(1)}, f32[256,4]{1,0:T(8,128)}, f32[256,4,128]{2,0,1:T(8,128)S(1)}) %tuple.31, (pred[512]{0:T(512)(128)(4,1)S(1)}, s32[512]{0:T(512)S(1)}, s32[256]{0:T(256)S(1)}, ...), branch_computations={%region_5.6_spmd, %region_6.9_spmd} | conditional | flops 273942784 | bytes 13486680 | solution.py:125
  114.2 0.5 broadcast_in_dim.64
  114.6 0.5 broadcast_in_dim.65
  115.1 1.5 fusion
  116.6 0.8 reduce_max.28
  117.4 1.6 max.12
  119.0 1.0 sub.66
  120.0 1.8 fusion.1
  122.0 1.7 multiply_add_fusion
  123.7 1.4 dot_general.9
  125.1 0.6 convolution_add_fusion
  125.7 4.8 conditional.3
  125.8 0.7 compare_and_fusion.1
  126.9 0.9 copy.56
  128.6 0.9 multiply_add_fusion.1
  130.6 0.5 collective-permute-start.3
  131.2 1.3 collective-permute-done.3
  132.6 0.6 collective-permute-start.6
  133.2 1.5 collective-permute-start.10
  134.7 0.5 collective-permute-start.5
  135.2 11.6 %collective-permute-done.10 = f32[256,4]{0,1:T(4,128)S(1)} collective-permute-done((f32[256,4]{0,1:T(4,128)S(1)}, f32[256,4]{0,1:T(4,128)S(1)}, u32[]{:S(2)}, u32[]{:S(2)}) %collective-permute-start.10) | collective-permute-done | bytes 4128 | tf_op jit(solution)/shard_map/ppermute | solution.py:20
  147.1 3.5 collective-permute-start.11
  150.7 11.1 %collective-permute-done.11 = f32[256,4]{0,1:T(4,128)S(1)} collective-permute-done((f32[256,4]{0,1:T(4,128)S(1)}, f32[256,4]{0,1:T(4,128)S(1)}, u32[]{:S(2)}, u32[]{:S(2)}) %collective-permute-start.11) | collective-permute-done | bytes 4128 | tf_op jit(solution)/shard_map/ppermute | solution.py:20
  162.0 0.6 constant_dynamic-slice_fusion
  162.7 12.8 %all_gather.27 = bf16[64,4096]{1,0:T(8,128)(2,1)S(1)} all-gather(bf16[64,1024]{1,0:T(8,128)(2,1)S(1)} %copy-done.14), channel_id=1, replica_groups=mesh['wide'=64,'narrow'=4] {'narrow'}, dimensions={1}, use_global_device_ids=true | all-gather | bytes 655360 | tf_op jit(solution)/shard_map/all_gather | solution.py:142
  175.5 61.0 %all-gather.9.cloned.1.call-done = bf16[256,4096]{0,1:T(8,128)(2,1)} async-done(((bf16[256,64]{0,1:T(8,128)(2,1)}), bf16[256,4096]{0,1:T(8,128)(2,1)}) %all-gather.9.cloned.1.call-update) | async-done | bytes 2097168 | tf_op jit(solution)/shard_map/all_gather | solution.py:54
  236.4 2.7 fusion.30
  239.2 0.5 all-gather.13.cloned.1.call-update
  239.8 0.5 all-gather.15.cloned.1.call-update
  240.3 0.5 all-gather.17.cloned.1.call-update
  240.9 73.8 %all-gather.11.cloned.1.call-done = bf16[256,4096]{0,1:T(8,128)(2,1)} async-done(((bf16[256,64]{0,1:T(8,128)(2,1)}), bf16[256,4096]{0,1:T(8,128)(2,1)}) %all-gather.11.cloned.1.call-update) | async-done | bytes 2097168 | tf_op jit(solution)/shard_map/all_gather | solution.py:54
  314.8 2.3 fusion.19
  317.1 27.2 %all-gather.13.cloned.1.call-done = bf16[224,4096]{1,0:T(8,128)(2,1)} async-done(((bf16[224,1024]{1,0:T(8,128)(2,1)}), bf16[224,4096]{1,0:T(8,128)(2,1)}) %all-gather.13.cloned.1.call-update) | async-done | bytes 1835024 | tf_op jit(solution)/shard_map/all_gather | solution.py:143
  344.4 2.3 fusion.31
  346.7 30.5 %all-gather.15.cloned.1.call-done = bf16[224,4096]{1,0:T(8,128)(2,1)} async-done(((bf16[224,1024]{1,0:T(8,128)(2,1)}), bf16[224,4096]{1,0:T(8,128)(2,1)}) %all-gather.15.cloned.1.call-update) | async-done | bytes 1835024 | tf_op jit(solution)/shard_map/all_gather | solution.py:144
  377.3 32.9 %all-gather.17.cloned.1.call-done = bf16[224,4096]{1,0:T(8,128)(2,1)} async-done(((bf16[224,1024]{1,0:T(8,128)(2,1)}), bf16[224,4096]{1,0:T(8,128)(2,1)}) %all-gather.17.cloned.1.call-update) | async-done | bytes 1835024 | tf_op jit(solution)/shard_map/all_gather | solution.py:145
  410.2 6.4 %convolution_bitcast_fusion = f32[4096,256]{1,0:T(8,128)} fusion(bf16[224,4096]{1,0:T(8,128)(2,1)} %all-gather.17.cloned.1.call-done, bf16[224,4096]{1,0:T(8,128)(2,1)} %all-gather.15.cloned.1.call-done, bf16[256,4096]{0,1:T(8,128)(2,1)S(1)} %copy-done, f32[4096]{0:T(1024)S(1)} %convert_element_type.105, f32[256]{0:T(256)S(1)} %add_rsqrt_fusion, ...), kind=kOutput, calls=%fused_computation.32 | convolution fusion | flops 944062464 | bytes 10208256 | tf_op jit(solution)/shard_map/dot_general | solution.py:202
  416.6 0.7 compare_and_fusion.2
  417.3 0.6 compare_select_fusion
  418.2 1.3 gather_fusion
  419.6 1.3 gather_fusion.1
  420.9 0.9 fusion.40
  421.9 139.7 %reduce-scatter.2.cloned.1.call-done = f32[64,256]{1,0:T(8,128)} async-done(((f32[4096,256]{1,0:T(8,128)}), f32[64,256]{1,0:T(8,128)}) %reduce-scatter.2.cloned.1.call-update) | async-done | bytes 65552 | tf_op jit(solution)/shard_map/reduce_scatter | solution.py:201
  561.6 1.5 fusion.52
  (103 shorter events, 5.4 us)
Async XLA Ops:
  7.2 83.9 %all-gather.7.cloned.1.call-start = ((), (), s32[]{:S(2)}) async-start(), calls=%async_computation.1 | async-start | bytes 2129920 | tf_op jit(solution)/shard_map/all_gather | solution.py:54
  7.9 228.5 %all-gather.9.cloned.1.call-start = ((), (), s32[]{:S(2)}) async-start(), calls=%async_computation.2 | async-start | bytes 2129920 | tf_op jit(solution)/shard_map/all_gather | solution.py:54
  91.0 2.3 copy-start.1
  94.2 4.3 collective-permute-start
  98.5 5.0 collective-permute-start.1
  103.6 7.8 %collective-permute-start.2 = (bf16[256,384]{0,1:T(8,128)(2,1)S(1)}, bf16[256,384]{0,1:T(8,128)(2,1)S(1)}, u32[]{:S(2)}, u32[]{:S(2)}) collective-permute-start(bf16[256,384]{0,1:T(8,128)(2,1)S(1)} %maximum_select_fusion.1), channel_id=1, source_target_pairs={{0,16},{16,0},{4,20},{20,4},{8,24},{24,8},{12,28},{28,12},{32,48},... | collective-permute-start | bytes 589832 | tf_op jit(solution)/shard_map/ppermute | solution.py:20
  112.6 1.3 copy-start.9
  112.6 1.3 copy-start.11
  121.8 3.3 copy-start.7
  123.7 2.0 copy-start.2
  125.7 4.1 copy-start.4
  130.5 2.0 collective-permute-start.4
  130.6 1.9 collective-permute-start.3
  131.1 1.4 collective-permute-start.9
  132.5 30.2 %copy-start.14 = (bf16[64,1024]{1,0:T(8,128)(2,1)S(1)}, bf16[64,1024]{1,0:T(8,128)(2,1)}, u32[]{:S(2)}) copy-start(bf16[64,1024]{1,0:T(8,128)(2,1)} %param.24) | copy-start | bytes 393220
  132.6 103.8 %copy-start.13 = (bf16[256,64]{0,1:T(8,128)(2,1)S(1)}, bf16[256,64]{0,1:T(8,128)(2,1)}, u32[]{:S(2)}) copy-start(bf16[256,64]{0,1:T(8,128)(2,1)} %param.17) | copy-start | bytes 98308
  132.6 14.2 %collective-permute-start.6 = (f32[256,4,128]{0,2,1:T(8,128)S(1)}, f32[256,4,128]{0,2,1:T(8,128)S(1)}, u32[]{:S(2)}, u32[]{:S(2)}) collective-permute-start(f32[256,4,128]{0,2,1:T(8,128)S(1)} %multiply_add_fusion.3), channel_id=1, source_target_pairs={{0,8},{8,0},{4,12},{12,4},{16,24},{24,16},{20,28},{28,20},{32,40},... | collective-permute-start | bytes 1572872 | tf_op jit(solution)/shard_map/ppermute | solution.py:20
  133.2 13.6 %collective-permute-start.10 = (f32[256,4]{0,1:T(4,128)S(1)}, f32[256,4]{0,1:T(4,128)S(1)}, u32[]{:S(2)}, u32[]{:S(2)}) collective-permute-start(f32[256,4]{0,1:T(4,128)S(1)} %get-tuple-element.243), channel_id=1, source_target_pairs={{0,8},{8,0},{4,12},{12,4},{16,24},{24,16},{20,28},{28,20},{32,40},... | collective-permute-start | bytes 12296 | tf_op jit(solution)/shard_map/ppermute | solution.py:20
  134.7 12.1 %collective-permute-start.5 = (f32[256,4]{0,1:T(4,128)S(1)}, f32[256,4]{0,1:T(4,128)S(1)}, u32[]{:S(2)}, u32[]{:S(2)}) collective-permute-start(f32[256,4]{0,1:T(4,128)S(1)} %get-tuple-element.246), channel_id=1, source_target_pairs={{0,8},{8,0},{4,12},{12,4},{16,24},{24,16},{20,28},{28,20},{32,40},... | collective-permute-start | bytes 12296 | tf_op jit(solution)/shard_map/ppermute | solution.py:20
  147.0 14.9 %collective-permute-start.8 = (f32[256,4,128]{0,2,1:T(8,128)S(1)}, f32[256,4,128]{0,2,1:T(8,128)S(1)}, u32[]{:S(2)}, u32[]{:S(2)}) collective-permute-start(f32[256,4,128]{0,2,1:T(8,128)S(1)} %multiply_add_fusion.2), channel_id=1, source_target_pairs={{0,16},{16,0},{4,20},{20,4},{8,24},{24,8},{12,28},{28,12},{32,48},... | collective-permute-start | bytes 1572872 | tf_op jit(solution)/shard_map/ppermute | solution.py:20
  147.1 14.8 %collective-permute-start.11 = (f32[256,4]{0,1:T(4,128)S(1)}, f32[256,4]{0,1:T(4,128)S(1)}, u32[]{:S(2)}, u32[]{:S(2)}) collective-permute-start(f32[256,4]{0,1:T(4,128)S(1)} %get-tuple-element.239), channel_id=1, source_target_pairs={{0,16},{16,0},{4,20},{20,4},{8,24},{24,8},{12,28},{28,12},{32,48},... | collective-permute-start | bytes 12296 | tf_op jit(solution)/shard_map/ppermute | solution.py:20
  150.6 11.3 %collective-permute-start.7 = (f32[256,4]{0,1:T(4,128)S(1)}, f32[256,4]{0,1:T(4,128)S(1)}, u32[]{:S(2)}, u32[]{:S(2)}) collective-permute-start(f32[256,4]{0,1:T(4,128)S(1)} %get-tuple-element.242), channel_id=1, source_target_pairs={{0,16},{16,0},{4,20},{20,4},{8,24},{24,8},{12,28},{28,12},{32,48},... | collective-permute-start | bytes 12296 | tf_op jit(solution)/shard_map/ppermute | solution.py:20
  162.6 152.1 %all-gather.11.cloned.1.call-start = ((), (), s32[]{:S(2)}) async-start(), calls=%async_computation.3 | async-start | bytes 2129920 | tf_op jit(solution)/shard_map/all_gather | solution.py:54
  175.5 65.5 %copy-start.15 = (bf16[4096]{0:T(1024)(128)(2,1)S(1)}, bf16[4096]{0:T(1024)(128)(2,1)}, u32[]{:S(2)}) copy-start(bf16[4096]{0:T(1024)(128)(2,1)} %param.22) | copy-start | bytes 24580
  239.1 105.2 %all-gather.13.cloned.1.call-start = ((), (), s32[]{:S(2)}) async-start(), calls=%async_computation.4 | async-start | bytes 2293760 | tf_op jit(solution)/shard_map/all_gather | solution.py:143
  239.7 137.5 %all-gather.15.cloned.1.call-start = ((), (), s32[]{:S(2)}) async-start(), calls=%async_computation.5 | async-start | bytes 2293760 | tf_op jit(solution)/shard_map/all_gather | solution.py:144
  240.3 169.9 %all-gather.17.cloned.1.call-start = ((), (), s32[]{:S(2)}) async-start(), calls=%async_computation.6 | async-start | bytes 2293760 | tf_op jit(solution)/shard_map/all_gather | solution.py:145
  240.9 320.7 %reduce-scatter.2.cloned.1.call-start = ((), (), s32[]{:S(2)}) async-start(), calls=%async_computation.7 | async-start | bytes 4259840 | tf_op jit(solution)/shard_map/reduce_scatter | solution.py:201
  314.8 29.6 %copy-start = (bf16[256,4096]{0,1:T(8,128)(2,1)S(1)}, bf16[256,4096]{0,1:T(8,128)(2,1)}, u32[]{:S(2)}) copy-start(bf16[256,4096]{0,1:T(8,128)(2,1)} %all-gather.11.cloned.1.call-done) | copy-start | bytes 6291460
  416.5 1.4 copy-start.3
  416.5 1.6 copy-start.10
  416.5 1.6 copy-start.12
  416.6 4.4 copy-start.5
  416.6 4.4 copy-start.6
  416.6 145.0 %copy-start.8 = (bf16[256,64]{0,1:T(8,128)(2,1)S(1)}, bf16[256,64]{0,1:T(8,128)(2,1)}, u32[]{:S(2)}) copy-start(bf16[256,64]{0,1:T(8,128)(2,1)} %fusion.30) | copy-start | bytes 98308
Sparse Core Ops, SparseCore 0:
  10.8 80.2 all-gather.6
  162.8 73.6 all-gather.8
  239.8 74.9 all-gather.10
  316.4 27.8 all-gather.12
  346.0 31.1 all-gather.14
  378.9 31.1 all-gather.16
  416.7 144.8 reduce-scatter.1
where the time goes:
time: 570 us
  waiting for transfers between devices  462 us (81%)
  blocking collectives  27.1 us (5%)
  other arithmetic  25.7 us (5%)
  between operations  16.5 us (3%)
  matrix products  14.7 us (3%)
  local copies, waits for them, and re-layouts  12.8 us (2%)
  starting transfers between devices  10.4 us (2%)
    all_gather x3, waiting for transfers between devices, gather_cols(): return lax.all_gather(block, 'wide', axis=1, tiled=True)  196 us
    reduce_scatter x1, waiting for transfers between devices, per_device(): lax.psum_scatter(lax.dot_general(down_full, activation, (((0,), (1,)), ((...  140 us
    ppermute x12, waiting for transfers between devices, partner(): return lax.ppermute(block, axis, route)  33.9 us
    all_gather x1, waiting for transfers between devices, per_device(): lax.all_gather(wdown, 'narrow', axis=1, tiled=True)  32.9 us
    all_gather x1, waiting for transfers between devices, per_device(): lax.all_gather(wup, 'narrow', axis=1, tiled=True)  30.5 us
    all_gather x1, waiting for transfers between devices, per_device(): lax.all_gather(wgate, 'narrow', axis=1, tiled=True)  27.2 us
    all_gather x1, blocking collectives, per_device(): lax.all_gather(wqkv, 'narrow', axis=1, tiled=True)  14.4 us
    all_gather x1, blocking collectives, per_device(): lax.all_gather(wo, 'narrow', axis=1, tiled=True)  12.8 us
  transfers between devices with their start and end apart: 19, of which 12 were waited for; matrix products, arithmetic and copies ran while one was open for 3% of the time, Pallas kernels for 0%

commit v1 on v0

--- a/solution.py
+++ b/solution.py
@@ -8,6 +8,22 @@
 HD = 128
 WINDOW = 4096
 NEG_FILL = -1e30
+
+
+def gather_around(x, axis, dim):
+    ways, here, step = (lax.axis_size(axis), lax.axis_index(axis), x.shape[dim])
+    shape = [n * ways if d == dim else n for d, n in enumerate(x.shape)]
+    full = lax.dynamic_update_slice_in_dim(jnp.zeros(shape, x.dtype), x, here * step, axis=dim)
+    going_up = going_down = x
+    for far in range(1, ways // 2 + 1):
+        going_up = lax.ppermute(going_up, axis, [(d, (d + 1) % ways) for d in range(ways)])
+        full = lax.dynamic_update_slice_in_dim(full, going_up, (here - far) % ways * step, axis=dim)
+        if 2 * far < ways:
+            going_down = lax.ppermute(going_down, axis, [(d, (d - 1) % ways) for d in range(ways)])
+            full = lax.dynamic_update_slice_in_dim(
+                full, going_down, (here + far) % ways * step, axis=dim
+            )
+    return full
 
 
 def partner(block, axis, stride):
@@ -140,7 +156,7 @@
     qkv_full, out_full, gate_full, up_full, down_full = (
         lax.all_gather(wqkv, "narrow", axis=1, tiled=True),
         lax.all_gather(wo, "narrow", axis=1, tiled=True),
-        lax.all_gather(wgate, "narrow", axis=1, tiled=True),
+        gather_around(wgate, "narrow", 1),
         lax.all_gather(wup, "narrow", axis=1, tiled=True),
         lax.all_gather(wdown, "narrow", axis=1, tiled=True),
     )

time: 570 us -> 538 us (0.944)
  waiting for transfers between devices: 462 us -> 421 us
    all_gather x1 -> x0, waiting for transfers between devices: 27.2 us -> none  [per_device(): lax.all_gather(wgate, 'narrow', axis=1, tiled=True)]
    all_gather x3, waiting for transfers between devices: 196 us -> 171 us  [gather_cols(): return lax.all_gather(block, 'wide', axis=1, tiled=True)]
    ppermute x0 -> x3, waiting for transfers between devices: none -> 17.1 us  [the longest x2 17 us: gather_around(): lax.ppermute(going_up, axis, [(d, (d + 1) % ways) for d in range(ways)])]
  transfers between devices with their start and end apart: 19 -> 21, of which waited for: 12 -> 13; matrix products, arithmetic and copies ran while one was open for 3% -> 5% of each run, Pallas kernels for 0% -> 0%
where the time goes in v1:
time: 538 us; the launch traced here: 537 us
  waiting for transfers between devices  421 us (78%)
  blocking collectives  27.3 us (5%)
  other arithmetic  25.3 us (5%)
  local copies, waits for them, and re-layouts  17.7 us (3%)
  between operations  16.4 us (3%)
  matrix products  14.7 us (3%)
  starting transfers between devices  13.9 us (3%)
    all_gather x3, waiting for transfers between devices, gather_cols(): return lax.all_gather(block, 'wide', axis=1, tiled=True)  171 us
    reduce_scatter x1, waiting for transfers between devices, per_device(): lax.psum_scatter(lax.dot_general(down_full, activation, (((0,), (1,)), ((...  140 us
    ppermute x12, waiting for transfers between devices, partner(): return lax.ppermute(block, axis, route)  33.9 us
    all_gather x1, waiting for transfers between devices, per_device(): lax.all_gather(wdown, 'narrow', axis=1, tiled=True)  30.5 us
    all_gather x1, waiting for transfers between devices, per_device(): lax.all_gather(wup, 'narrow', axis=1, tiled=True)  27.2 us
    ppermute x2, waiting for transfers between devices, gather_around(): lax.ppermute(going_up, axis, [(d, (d + 1) % ways) for d in range(ways)])  17 us
    all_gather x1, blocking collectives, per_device(): lax.all_gather(wqkv, 'narrow', axis=1, tiled=True)  14.4 us
    all_gather x1, blocking collectives, per_device(): lax.all_gather(wo, 'narrow', axis=1, tiled=True)  12.9 us
  transfers between devices with their start and end apart: 21, of which 13 were waited for; matrix products, arithmetic and copies ran while one was open for 5% of the time, Pallas kernels for 0%

profile of v1, /device:TPU:2, one launch (start us, length us, event | category | flops | bytes accessed | tf_op | source)
XLA Modules:
  0.0 536.9 jit_solution(6991245326974893274)
XLA Ops:
  7.2 0.7 all-gather.6.cloned.1.call-update
  8.0 1.2 dynamic_slice.37
  9.2 1.2 fusion.61
  10.4 1.2 fusion.62
  11.6 0.7 convert_element_type.93
  12.9 1.9 fusion.56
  14.8 0.6 iota_add_fusion.1
  15.4 14.4 %all_gather.22 = bf16[96,4096]{1,0:T(8,128)(2,1)S(1)} all-gather(bf16[96,1024]{1,0:T(8,128)(2,1)} %param.23), channel_id=1, replica_groups=mesh['wide'=64,'narrow'=4] {'narrow'}, dimensions={1}, use_global_device_ids=true | all-gather | bytes 983040 | tf_op jit(solution)/shard_map/all_gather | solution.py:157
  29.7 61.3 %all-gather.6.cloned.1.call-done = bf16[256,4096]{0,1:T(8,128)(2,1)} async-done(((bf16[256,64]{0,1:T(8,128)(2,1)}), bf16[256,4096]{0,1:T(8,128)(2,1)}) %all-gather.6.cloned.1.call-update) | async-done | bytes 2097168 | tf_op jit(solution)/shard_map/all_gather | solution.py:70
  91.0 2.3 fusion.16
  93.4 0.8 fusion.26
  94.6 1.9 and_reduce_fusion
  97.8 0.7 broadcast_in_dim.117
  98.4 0.6 collective-permute-start.1
  99.1 4.4 collective-permute-done.1
  103.5 2.2 collective-permute-start.2
  106.0 5.3 collective-permute-done.2
  111.5 0.6 fusion.67
  113.0 0.6 pad_maximum_fusion.1
  113.8 11.8 %conditional.2 = ((f32[256,4]{1,0:T(8,128)S(1)}, f32[256,4]{1,0:T(8,128)}, f32[256,4,128]{2,0,1:T(8,128)S(1)})) conditional(s32[]{:T(128)} %convert_element_type.91, (f32[256,4]{1,0:T(8,128)S(1)}, f32[256,4]{1,0:T(8,128)}, f32[256,4,128]{2,0,1:T(8,128)S(1)}) %tuple.31, (pred[512]{0:T(512)(128)(4,1)S(1)}, s32[512]{0:T(512)S(1)}, s32[256]{0:T(256)S(1)}, ...), branch_computations={%region_5.6_spmd, %region_6.9_spmd} | conditional | flops 273942784 | bytes 13486680 | solution.py:141
  115.1 1.5 fusion
  116.5 0.8 reduce_max.28
  117.3 1.6 max.12
  118.9 1.0 sub.70
  119.9 1.8 fusion.1
  121.9 1.7 multiply_add_fusion
  123.6 1.4 dot_general.9
  125.0 0.6 convolution_add_fusion
  125.6 4.8 conditional.3
  125.7 0.7 compare_and_fusion.1
  126.9 0.9 copy.56
  128.5 0.9 multiply_add_fusion.1
  131.1 1.3 collective-permute-done.3
  132.6 0.6 collective-permute-start.6
  133.1 1.5 collective-permute-start.10
  135.2 11.6 %collective-permute-done.10 = f32[256,4]{0,1:T(4,128)S(1)} collective-permute-done((f32[256,4]{0,1:T(4,128)S(1)}, f32[256,4]{0,1:T(4,128)S(1)}, u32[]{:S(2)}, u32[]{:S(2)}) %collective-permute-start.10) | collective-permute-done | bytes 4128 | tf_op jit(solution)/shard_map/ppermute | solution.py:36
  147.0 3.5 collective-permute-start.11
  150.6 11.1 %collective-permute-done.11 = f32[256,4]{0,1:T(4,128)S(1)} collective-permute-done((f32[256,4]{0,1:T(4,128)S(1)}, f32[256,4]{0,1:T(4,128)S(1)}, u32[]{:S(2)}, u32[]{:S(2)}) %collective-permute-start.11) | collective-permute-done | bytes 4128 | tf_op jit(solution)/shard_map/ppermute | solution.py:36
  161.9 0.6 constant_dynamic-slice_fusion
  162.6 12.9 %all_gather.24 = bf16[64,4096]{1,0:T(8,128)(2,1)S(1)} all-gather(bf16[64,1024]{1,0:T(8,128)(2,1)S(1)} %copy-done.15), channel_id=1, replica_groups=mesh['wide'=64,'narrow'=4] {'narrow'}, dimensions={1}, use_global_device_ids=true | all-gather | bytes 655360 | tf_op jit(solution)/shard_map/all_gather | solution.py:158
  175.5 60.8 %all-gather.8.cloned.1.call-done = bf16[256,4096]{0,1:T(8,128)(2,1)} async-done(((bf16[256,64]{0,1:T(8,128)(2,1)}), bf16[256,4096]{0,1:T(8,128)(2,1)}) %all-gather.8.cloned.1.call-update) | async-done | bytes 2097168 | tf_op jit(solution)/shard_map/all_gather | solution.py:70
  236.4 2.7 fusion.29
  240.3 1.5 collective-permute-start.12
  242.4 10.7 %collective-permute-done.12 = bf16[224,1024]{1,0:T(8,128)(2,1)S(1)} collective-permute-done((bf16[224,1024]{1,0:T(8,128)(2,1)S(1)}, bf16[224,1024]{1,0:T(8,128)(2,1)S(1)}, u32[]{:S(2)}, u32[]{:S(2)}) %collective-permute-start.12) | collective-permute-done | bytes 458784 | tf_op jit(solution)/shard_map/ppermute | solution.py:19
  253.1 1.5 collective-permute-start.14
  254.5 1.5 broadcast_in_dim.119
  256.0 0.9 constant_dynamic-update-slice_fusion.3
  256.9 0.8 constant_dynamic-update-slice_fusion.2
  257.7 0.8 constant_dynamic-update-slice_fusion.1
  258.6 6.4 %collective-permute-done.14 = bf16[224,1024]{1,0:T(8,128)(2,1)S(1)} collective-permute-done((bf16[224,1024]{1,0:T(8,128)(2,1)S(1)}, bf16[224,1024]{1,0:T(8,128)(2,1)S(1)}, u32[]{:S(2)}, u32[]{:S(2)}) %collective-permute-start.14) | collective-permute-done | bytes 458784 | tf_op jit(solution)/shard_map/ppermute | solution.py:19
  265.0 0.9 constant_dynamic-update-slice_fusion
  265.8 48.9 %all-gather.10.cloned.1.call-done = bf16[256,4096]{0,1:T(8,128)(2,1)} async-done(((bf16[256,64]{0,1:T(8,128)(2,1)}), bf16[256,4096]{0,1:T(8,128)(2,1)}) %all-gather.10.cloned.1.call-update) | async-done | bytes 2097168 | tf_op jit(solution)/shard_map/all_gather | solution.py:70
  314.7 2.3 fusion.19
  317.0 27.2 %all-gather.12.cloned.1.call-done = bf16[224,4096]{1,0:T(8,128)(2,1)} async-done(((bf16[224,1024]{1,0:T(8,128)(2,1)}), bf16[224,4096]{1,0:T(8,128)(2,1)}) %all-gather.12.cloned.1.call-update) | async-done | bytes 1835024 | tf_op jit(solution)/shard_map/all_gather | solution.py:160
  344.3 2.4 fusion.32
  346.6 30.5 %all-gather.14.cloned.1.call-done = bf16[224,4096]{1,0:T(8,128)(2,1)} async-done(((bf16[224,1024]{1,0:T(8,128)(2,1)}), bf16[224,4096]{1,0:T(8,128)(2,1)}) %all-gather.14.cloned.1.call-update) | async-done | bytes 1835024 | tf_op jit(solution)/shard_map/all_gather | solution.py:161
  377.2 6.4 %convolution_bitcast_fusion = f32[4096,256]{1,0:T(8,128)} fusion(bf16[224,4096]{1,0:T(8,128)(2,1)} %all-gather.14.cloned.1.call-done, f32[256,224]{0,1:T(8,128)S(1)} %fusion.32, bf16[224,4096]{1,0:T(8,128)(2,1)} %constant_dynamic-update-slice_fusion, bf16[256,4096]{0,1:T(8,128)(2,1)S(1)} %copy-done, f32[4096]{0:T(1024)S(1)} %convert_element_type.105, ...), kind=kOutput, calls=%fused_computation.32 | convolution fusion | flops 944062464 | bytes 10208256 | tf_op jit(solution)/shard_map/dot_general | solution.py:218
  383.6 0.7 compare_and_fusion.2
  384.3 0.6 compare_select_fusion
  385.2 1.3 gather_fusion
  386.5 1.3 gather_fusion.1
  387.9 0.9 fusion.38
  388.8 139.9 %reduce-scatter.2.cloned.1.call-done = f32[64,256]{1,0:T(8,128)} async-done(((f32[4096,256]{1,0:T(8,128)}), f32[64,256]{1,0:T(8,128)}) %reduce-scatter.2.cloned.1.call-update) | async-done | bytes 65552 | tf_op jit(solution)/shard_map/reduce_scatter | solution.py:217
  528.6 1.5 fusion.50
  (113 shorter events, 9.3 us)
Async XLA Ops:
  7.2 83.9 %all-gather.6.cloned.1.call-start = ((), (), s32[]{:S(2)}) async-start(), calls=%async_computation.1 | async-start | bytes 2129920 | tf_op jit(solution)/shard_map/all_gather | solution.py:70
  7.9 228.5 %all-gather.8.cloned.1.call-start = ((), (), s32[]{:S(2)}) async-start(), calls=%async_computation.2 | async-start | bytes 2129920 | tf_op jit(solution)/shard_map/all_gather | solution.py:70
  91.0 2.3 copy-start.1
  94.2 4.2 collective-permute-start
  98.4 5.0 collective-permute-start.1
  103.5 7.8 %collective-permute-start.2 = (bf16[256,384]{0,1:T(8,128)(2,1)S(1)}, bf16[256,384]{0,1:T(8,128)(2,1)S(1)}, u32[]{:S(2)}, u32[]{:S(2)}) collective-permute-start(bf16[256,384]{0,1:T(8,128)(2,1)S(1)} %maximum_select_fusion.1), channel_id=1, source_target_pairs={{0,16},{16,0},{4,20},{20,4},{8,24},{24,8},{12,28},{28,12},{32,48},... | collective-permute-start | bytes 589832 | tf_op jit(solution)/shard_map/ppermute | solution.py:36
  112.5 1.3 copy-start.10
  112.5 1.3 copy-start.12
  121.7 3.3 copy-start.7
  123.6 2.0 copy-start.2
  125.6 4.1 copy-start.4
  130.4 2.0 collective-permute-start.4
  130.5 1.9 collective-permute-start.3
  131.0 1.4 collective-permute-start.9
  132.4 30.2 %copy-start.15 = (bf16[64,1024]{1,0:T(8,128)(2,1)S(1)}, bf16[64,1024]{1,0:T(8,128)(2,1)}, u32[]{:S(2)}) copy-start(bf16[64,1024]{1,0:T(8,128)(2,1)} %param.24) | copy-start | bytes 393220
  132.5 103.8 %copy-start.14 = (bf16[256,64]{0,1:T(8,128)(2,1)S(1)}, bf16[256,64]{0,1:T(8,128)(2,1)}, u32[]{:S(2)}) copy-start(bf16[256,64]{0,1:T(8,128)(2,1)} %param.17) | copy-start | bytes 98308
  132.6 14.2 %collective-permute-start.6 = (f32[256,4,128]{0,2,1:T(8,128)S(1)}, f32[256,4,128]{0,2,1:T(8,128)S(1)}, u32[]{:S(2)}, u32[]{:S(2)}) collective-permute-start(f32[256,4,128]{0,2,1:T(8,128)S(1)} %multiply_add_fusion.3), channel_id=1, source_target_pairs={{0,8},{8,0},{4,12},{12,4},{16,24},{24,16},{20,28},{28,20},{32,40},... | collective-permute-start | bytes 1572872 | tf_op jit(solution)/shard_map/ppermute | solution.py:36
  133.1 13.6 %collective-permute-start.10 = (f32[256,4]{0,1:T(4,128)S(1)}, f32[256,4]{0,1:T(4,128)S(1)}, u32[]{:S(2)}, u32[]{:S(2)}) collective-permute-start(f32[256,4]{0,1:T(4,128)S(1)} %get-tuple-element.243), channel_id=1, source_target_pairs={{0,8},{8,0},{4,12},{12,4},{16,24},{24,16},{20,28},{28,20},{32,40},... | collective-permute-start | bytes 12296 | tf_op jit(solution)/shard_map/ppermute | solution.py:36
  134.7 12.1 %collective-permute-start.5 = (f32[256,4]{0,1:T(4,128)S(1)}, f32[256,4]{0,1:T(4,128)S(1)}, u32[]{:S(2)}, u32[]{:S(2)}) collective-permute-start(f32[256,4]{0,1:T(4,128)S(1)} %get-tuple-element.246), channel_id=1, source_target_pairs={{0,8},{8,0},{4,12},{12,4},{16,24},{24,16},{20,28},{28,20},{32,40},... | collective-permute-start | bytes 12296 | tf_op jit(solution)/shard_map/ppermute | solution.py:36
  146.9 14.9 %collective-permute-start.8 = (f32[256,4,128]{0,2,1:T(8,128)S(1)}, f32[256,4,128]{0,2,1:T(8,128)S(1)}, u32[]{:S(2)}, u32[]{:S(2)}) collective-permute-start(f32[256,4,128]{0,2,1:T(8,128)S(1)} %multiply_add_fusion.2), channel_id=1, source_target_pairs={{0,16},{16,0},{4,20},{20,4},{8,24},{24,8},{12,28},{28,12},{32,48},... | collective-permute-start | bytes 1572872 | tf_op jit(solution)/shard_map/ppermute | solution.py:36
  147.0 14.8 %collective-permute-start.11 = (f32[256,4]{0,1:T(4,128)S(1)}, f32[256,4]{0,1:T(4,128)S(1)}, u32[]{:S(2)}, u32[]{:S(2)}) collective-permute-start(f32[256,4]{0,1:T(4,128)S(1)} %get-tuple-element.239), channel_id=1, source_target_pairs={{0,16},{16,0},{4,20},{20,4},{8,24},{24,8},{12,28},{28,12},{32,48},... | collective-permute-start | bytes 12296 | tf_op jit(solution)/shard_map/ppermute | solution.py:36
  150.5 11.3 %collective-permute-start.7 = (f32[256,4]{0,1:T(4,128)S(1)}, f32[256,4]{0,1:T(4,128)S(1)}, u32[]{:S(2)}, u32[]{:S(2)}) collective-permute-start(f32[256,4]{0,1:T(4,128)S(1)} %get-tuple-element.242), channel_id=1, source_target_pairs={{0,16},{16,0},{4,20},{20,4},{8,24},{24,8},{12,28},{28,12},{32,48},... | collective-permute-start | bytes 12296 | tf_op jit(solution)/shard_map/ppermute | solution.py:36
  162.6 77.7 %copy-start.8 = (bf16[224,1024]{1,0:T(8,128)(2,1)S(1)}, bf16[224,1024]{1,0:T(8,128)(2,1)}, u32[]{:S(2)}) copy-start(bf16[224,1024]{1,0:T(8,128)(2,1)} %param.25) | copy-start | bytes 1376260
  162.6 92.0 %copy-start.16 = (bf16[4096]{0:T(1024)(128)(2,1)S(1)}, bf16[4096]{0:T(1024)(128)(2,1)}, u32[]{:S(2)}) copy-start(bf16[4096]{0:T(1024)(128)(2,1)} %param.22) | copy-start | bytes 24580
  162.6 152.1 %all-gather.10.cloned.1.call-start = ((), (), s32[]{:S(2)}) async-start(), calls=%async_computation.3 | async-start | bytes 2129920 | tf_op jit(solution)/shard_map/all_gather | solution.py:70
  239.1 105.2 %all-gather.12.cloned.1.call-start = ((), (), s32[]{:S(2)}) async-start(), calls=%async_computation.4 | async-start | bytes 2293760 | tf_op jit(solution)/shard_map/all_gather | solution.py:160
  239.6 137.5 %all-gather.14.cloned.1.call-start = ((), (), s32[]{:S(2)}) async-start(), calls=%async_computation.5 | async-start | bytes 2293760 | tf_op jit(solution)/shard_map/all_gather | solution.py:161
  240.2 288.4 %reduce-scatter.2.cloned.1.call-start = ((), (), s32[]{:S(2)}) async-start(), calls=%async_computation.6 | async-start | bytes 4259840 | tf_op jit(solution)/shard_map/reduce_scatter | solution.py:217
  240.3 12.8 %collective-permute-start.12 = (bf16[224,1024]{1,0:T(8,128)(2,1)S(1)}, bf16[224,1024]{1,0:T(8,128)(2,1)S(1)}, u32[]{:S(2)}, u32[]{:S(2)}) collective-permute-start(bf16[224,1024]{1,0:T(8,128)(2,1)S(1)} %copy-done.8), channel_id=1, source_target_pairs={{0,1},{1,2},{2,3},{3,0},{4,5},{5,6},{6,7},{7,4},{8,9},{9,10},{10,1... | collective-permute-start | bytes 1376264 | tf_op jit(solution)/shard_map/ppermute | solution.py:19
  241.8 15.9 %collective-permute-start.13 = (bf16[224,1024]{1,0:T(8,128)(2,1)S(1)}, bf16[224,1024]{1,0:T(8,128)(2,1)S(1)}, u32[]{:S(2)}, u32[]{:S(2)}) collective-permute-start(bf16[224,1024]{1,0:T(8,128)(2,1)S(1)} %copy-done.8), channel_id=1, source_target_pairs={{0,3},{1,0},{2,1},{3,2},{4,7},{5,4},{6,5},{7,6},{8,11},{9,8},{10,9... | collective-permute-start | bytes 1376264 | tf_op jit(solution)/shard_map/ppermute | solution.py:22
  253.1 11.9 %collective-permute-start.14 = (bf16[224,1024]{1,0:T(8,128)(2,1)S(1)}, bf16[224,1024]{1,0:T(8,128)(2,1)S(1)}, u32[]{:S(2)}, u32[]{:S(2)}) collective-permute-start(bf16[224,1024]{1,0:T(8,128)(2,1)S(1)} %collective-permute-done.12), channel_id=1, source_target_pairs={{0,1},{1,2},{2,3},{3,0},{4,5},{5,6},{6,7},{7,4},{8,9},{9,10},{10,1... | collective-permute-start | bytes 1376264 | tf_op jit(solution)/shard_map/ppermute | solution.py:19
  314.7 29.6 %copy-start = (bf16[256,4096]{0,1:T(8,128)(2,1)S(1)}, bf16[256,4096]{0,1:T(8,128)(2,1)}, u32[]{:S(2)}) copy-start(bf16[256,4096]{0,1:T(8,128)(2,1)} %all-gather.10.cloned.1.call-done) | copy-start | bytes 6291460
  383.6 1.3 copy-start.3
  383.6 1.4 copy-start.11
  383.6 1.5 copy-start.13
  383.6 4.3 copy-start.5
  383.6 4.3 copy-start.6
  383.6 145.0 %copy-start.9 = (bf16[256,64]{0,1:T(8,128)(2,1)S(1)}, bf16[256,64]{0,1:T(8,128)(2,1)}, u32[]{:S(2)}) copy-start(bf16[256,64]{0,1:T(8,128)(2,1)} %fusion.29) | copy-start | bytes 98308
Sparse Core Ops, SparseCore 0:
  10.8 80.2 all-gather.5
  162.7 73.6 all-gather.7
  239.7 74.9 all-gather.9
  316.4 27.8 all-gather.11
  345.9 31.1 all-gather.13
  383.7 144.8 reduce-scatter.1
